TPU v7x, 128 devices: a whole 4x4x4 slice. The times are simulated.
128 devices in a mesh: row: 8 (over x_lo, z), col: 16 (over x_hi, y, core).
Axes of the slice: x: 4 (x_hi: 2, x_lo: 2; x = x_hi * 2 + x_lo), y: 4, z: 4, core: 2. Of those that a mesh axis runs over, the one named last changes fastest.
Arguments:
- amplitudes: bfloat16 [16384, 2048], P(('row', 'col')), may hold values from -6 to 6
- integrals: bfloat16 [2048, 49152], P('row', 'col'), may hold values from -0.125 to 0.125
Outputs:
- ladder: bfloat16 [16384, 49152], P(('row', 'col'))
All inputs are finite; a program needn't handle non-finite values.
Results may differ from a plain program's by a relative error of at most 0.001.
Values may be sent and summed in bfloat16 or wider, within the bound.
A program may use at most 128 MiB of HBM per device.

v0:
```python
import jax
import jax.numpy as jnp
from jax import lax
from jax.sharding import PartitionSpec as P


def body(amplitudes, integrals):
    columns = lax.all_gather(integrals, "row", axis=0, tiled=True)
    block_amps = lax.all_to_all(amplitudes, "col", split_axis=1, concat_axis=0, tiled=True)
    ladder_block = jnp.dot(
        lax.all_gather(block_amps, "col", axis=1, tiled=True),
        columns,
        preferred_element_type=jnp.float32,
    )
    rounded = ladder_block.astype(jnp.bfloat16)
    return lax.all_to_all(rounded, "col", split_axis=0, concat_axis=1, tiled=True)


def solution(mesh):
    placed = (P(("row", "col"), None), P("row", "col"))
    return jax.shard_map(
        body, mesh=mesh, in_specs=placed, out_specs=P(("row", "col"), None), check_vma=False
    )
```

profile of v0, /device:TPU:1, one launch (start us, length us, event | category | flops | bytes accessed | tf_op | source)
XLA Modules:
  0.0 424.6 jit_solution(12910131834095765068)
XLA Ops:
  6.5 0.0 all-gather.3.cloned.1.call-start
  6.5 1.3 copy.5
  7.9 19.4 %all_to_all.38 = bf16[128,16,128]{0,2,1:T(8,128)(2,1)S(1)} all-to-all(bf16[128,16,128]{0,2,1:T(8,128)(2,1)S(1)} %bitcast.13), channel_id=1, replica_groups=mesh['row'=8,'col'=16] {'col'}, dimensions={1} | all-to-all | bytes 1048576 | tf_op jit(solution)/shard_map/all_to_all | solution.py:9
  27.2 1.0 copy.6
  28.3 0.0 all-gather.3.cloned.1.call-update
  28.3 0.0 all-gather.5.cloned.1.call-start
  28.3 0.7 all-gather.5.cloned.1.call-update
  29.0 74.8 %all-gather.3.cloned.1.call-done = bf16[2048,2048]{1,0:T(8,128)(2,1)} async-done(((bf16[2048,128]{1,0:T(8,128)(2,1)}), bf16[2048,2048]{1,0:T(8,128)(2,1)}) %all-gather.3.cloned.1.call-update) | async-done | bytes 8388624 | tf_op jit(solution)/shard_map/all_gather | solution.py:11
  103.8 130.0 %all-gather.5.cloned.1.call-done = bf16[2048,3072]{1,0:T(8,128)(2,1)} async-done(((bf16[256,3072]{1,0:T(8,128)(2,1)}), bf16[2048,3072]{1,0:T(8,128)(2,1)}) %all-gather.5.cloned.1.call-update) | async-done | bytes 12582928 | tf_op jit(solution)/shard_map/all_gather | solution.py:8
  233.9 31.3 %convolution_convert_fusion = bf16[2048,3072]{1,0:T(8,128)(2,1)S(1)} fusion(bf16[2048,2048]{1,0:T(8,128)(2,1)} %all-gather.3.cloned.1.call-done, bf16[2048,3072]{1,0:T(8,128)(2,1)} %all-gather.5.cloned.1.call-done), kind=kOutput, calls=%fused_computation | convolution fusion | flops 25776095232 | bytes 33554432 | tf_op jit(solution)/shard_map/dot_general | solution.py:10
  265.2 147.4 %all_to_all.39 = bf16[16,128,3072]{2,1,0:T(8,128)(2,1)S(1)} all-to-all(bf16[16,128,3072]{2,1,0:T(8,128)(2,1)S(1)} %bitcast.10), channel_id=1, replica_groups=mesh['row'=8,'col'=16] {'col'}, dimensions={0} | all-to-all | bytes 25165824 | tf_op jit(solution)/shard_map/all_to_all | solution.py:16
  412.6 5.2 %copy.8 = bf16[16,16,8,3072]{3,2,0,1:T(8,128)(2,1)} copy(bf16[16,16,8,3072]{3,2,1,0:T(8,128)(2,1)S(1)} %bitcast.9) | data formatting | bytes 25165824 | tf_op jit(solution)/shard_map/all_to_all | solution.py:16
Async XLA Ops:
  6.5 97.3 %all-gather.3.cloned.1.call-start = ((), (), s32[]{:S(2)}) async-start(), calls=%async_computation.2 | async-start | bytes 8912896 | tf_op jit(solution)/shard_map/all_gather | solution.py:11
  28.3 205.6 %all-gather.5.cloned.1.call-start = ((), (), s32[]{:S(2)}) async-start(), calls=%async_computation.3 | async-start | bytes 14155776 | tf_op jit(solution)/shard_map/all_gather | solution.py:8
Sparse Core Ops, SparseCore 0:
  28.4 75.3 all-gather.2
  105.5 128.3 all-gather.4
where the time goes:
time: 425 us
  waiting for transfers between devices  206 us (48%)
  blocking collectives  167 us (39%)
  matrix products  31.3 us (7%)
  between operations  13.4 us (3%)
  local copies, waits for them, and re-layouts  7.48 us (2%)
    all_to_all x1, blocking collectives, body(): lax.all_to_all(rounded, 'col', split_axis=0, concat_axis=1, tiled=True)  147 us
    all_gather x1, waiting for transfers between devices, body(): columns = lax.all_gather(integrals, 'row', axis=0, tiled=True)  130 us
    all_gather x1, waiting for transfers between devices, body(): lax.all_gather(block_amps, 'col', axis=1, tiled=True)  74.8 us
    dot_general x1, matrix products, body(): jnp.dot(lax.all_gather(block_amps, 'col', axis=1, tiled=True), columns, p...  31.3 us
    all_to_all x1, blocking collectives, body(): lax.all_to_all(amplitudes, 'col', split_axis=1, concat_axis=0, tiled=True)  19.4 us
  transfers between devices with their start and end apart: 2, of which 2 were waited for; matrix products, arithmetic and copies ran while one was open for 0% of the time, Pallas kernels for 0%

commit v1 on v0

v1 whole, which is shorter than its diff:
```python
import functools

import jax
import jax.numpy as jnp
from jax import lax
from jax.experimental import pallas as pl
from jax.experimental.pallas import tpu as pltpu
from jax.sharding import PartitionSpec as P

MESH = pl.DeviceIdType.MESH
W = 128


def kernel(steps, amps, ints, out, a_all, b_all, o_all, a_near, a_far, a_core, a_send, b_one, b_two, b_three, b_send, o_recv, o_send):
    row, col = lax.axis_index("row"), lax.axis_index("col")
    hi, lo, y, z, core = col // 8, row // 4, (col // 2) % 4, row % 4, col % 2
    x = hi * 2 + lo

    def at(x, y, z, core):
        return ((x % 2) * 4 + z, (x // 2) * 8 + y * 2 + core)

    def turn(v, by):
        return (v + by) % 4

    def send(src, dst, send_sem, recv_sem, device):
        return pltpu.make_async_remote_copy(
            src_ref=src, dst_ref=dst, send_sem=send_sem, recv_sem=recv_sem, device_id=device, device_id_type=MESH
        )

    def await_bytes(ref, sem):
        pltpu.make_async_copy(ref, ref, sem).wait()

    barrier = pltpu.get_barrier_semaphore()
    ring = [1, 3, 2]
    partners = [at(turn(x, d), y, z, core) for d in ring] + [at(x, y, turn(z, d), core) for d in ring]
    partners += [at(x, turn(y, d), z, core) for d in ring] + [at(x, turn(y, d), z, 1 - core) for d in [0] + ring]
    for device in partners:
        pl.semaphore_signal(barrier, inc=1, device_id=device, device_id_type=MESH)
    pl.semaphore_wait(barrier, len(partners))

    def half(i):
        return pl.ds(pl.multiple_of(i * W, W), W)

    def one(j):
        cols = half(j)
        for d in ring:
            send(ints.at[0, :, cols], b_all.at[j, lo, z, 0, :, half(hi)], b_send.at[j], b_one.at[j], at(turn(x, d), y, z, core)).start()
            send(ints.at[1, :, cols], b_all.at[j, lo, z, 1, :, half(hi)], b_send.at[j], b_one.at[j], at(x, y, turn(z, d), core)).start()
        pltpu.make_async_copy(ints.at[:, :, cols], b_all.at[j, lo, z, :, :, half(hi)], b_one.at[j]).start()

    def two(j):
        await_bytes(b_all.at[j, 0, :, 0], b_one.at[j])
        for d in (1, 3):
            block = b_all.at[j, :, z, 0]
            send(block, block, b_send.at[j], b_two.at[j], at(x, y, turn(z, d), core)).start()
            block = b_all.at[j, lo, :, 1, :, half(hi)]
            send(block, block, b_send.at[j], b_two.at[j], at(turn(x, d), y, z, core)).start()

    def three(j):
        await_bytes(b_all.at[j, :, :, 0], b_two.at[j])
        for i, d in enumerate((1, 3)):
            block = b_all.at[j, i, turn(z, 4 - d), 0]
            send(block, block, b_send.at[j], b_three.at[j], at(x, y, turn(z, d), core)).start()
            source = turn(x, 4 - d)
            block = b_all.at[j, source % 2, pl.ds(2 * i, 2), 1, :, half(source // 2)]
            send(block, block, b_send.at[j], b_three.at[j], at(turn(x, d), y, z, core)).start()

    def deliver(j, y_to):
        for k in range(2):
            for h in range(2):
                src = o_all.at[j, y_to, pl.ds(k * 128, 128), pl.ds(h * W, W)]
                dst = out.at[:, pl.ds(pl.multiple_of((h * 8 + y * 2 + core) * (steps * W) + j * W, W), W)]
                own = jnp.logical_and(y_to == y, core == k)

                @pl.when(own)
                def _():
                    pltpu.make_async_copy(src, dst, o_recv.at[j]).start()

                @pl.when(jnp.logical_not(own))
                def _():
                    send(src, dst, o_send.at[j], o_recv.at[j], at(x, y_to, z, k)).start()

    def compute(j):
        await_bytes(b_all.at[j, 0, :, 0], b_three.at[j])

        def tile(m, _):
            y_to = turn(y, m + 2)
            block = jnp.dot(
                a_all[pl.ds(2 * y_to, 2)].reshape(256, 2048), b_all[j].reshape(16 * 128, 2 * W), preferred_element_type=jnp.float32
            )
            o_all[j, y_to] = block.astype(jnp.bfloat16)
            deliver(j, y_to)
            return 0

        lax.fori_loop(0, 4, tile, 0)

    mine = a_all.at[2 * y + core]

    def amplitudes_start():
        pltpu.make_async_copy(amps, mine, a_core).start()
        send(amps, mine, a_send, a_near, at(x, turn(y, 1), z, core)).start()
        send(amps, mine, a_send, a_near, at(x, turn(y, 3), z, core)).start()
        send(amps, mine, a_send, a_far, at(x, turn(y, 2), z, core)).start()
        send(amps, mine, a_send, a_core, at(x, y, z, 1 - core)).start()

    def to_core(y_of):
        block = a_all.at[2 * y_of + core]
        send(block, block, a_send, a_core, at(x, y, z, 1 - core)).start()

    def step(t, _):
        @pl.when(jnp.logical_and(t >= 2, t < steps + 2))
        def _():
            three(t - 2)

        @pl.when(jnp.logical_and(t >= 1, t < steps + 1))
        def _():
            two(t - 1)

        @pl.when(t < steps)
        def _():
            one(t)

        @pl.when(t == 0)
        def _():
            amplitudes_start()

        @pl.when(t == 2)
        def _():
            await_bytes(a_all.at[pl.ds(0, 2)], a_near)
            to_core(turn(y, 1))
            to_core(turn(y, 3))

        @pl.when(t == 3)
        def _():
            await_bytes(a_all.at[0], a_far)
            to_core(turn(y, 2))
            await_bytes(a_all.at[pl.ds(0, 5)], a_core)

        @pl.when(t >= 3)
        def _():
            compute(t - 3)

        return 0

    lax.fori_loop(0, steps + 3, step, 0)

    await_bytes(a_all.at[pl.ds(0, 7)], a_send)

    def drain(j, _):
        await_bytes(out.at[:, pl.ds(0, 30 * W)], b_send.at[j])
        await_bytes(out.at[pl.ds(0, 112), pl.ds(0, 16 * W)], o_send.at[j])
        await_bytes(out.at[:, pl.ds(0, 16 * W)], o_recv.at[j])
        return 0

    lax.fori_loop(0, steps, drain, 0)


def body(amplitudes, integrals):
    depth, width = integrals.shape
    steps = width // W
    sem = pltpu.SemaphoreType.DMA
    return pl.pallas_call(
        functools.partial(kernel, steps),
        out_shape=jax.ShapeDtypeStruct((128, 16 * width), jnp.bfloat16),
        in_specs=[pl.BlockSpec(memory_space=pl.ANY)] * 2,
        out_specs=pl.BlockSpec(memory_space=pl.ANY),
        scratch_shapes=[
            pltpu.VMEM((8, 128, 2048), jnp.bfloat16),
            pltpu.VMEM((steps, 2, 4, 2, 128, 2 * W), jnp.bfloat16),
            pltpu.VMEM((steps, 4, 256, 2 * W), jnp.bfloat16),
            sem, sem, sem, sem,
            sem((steps,)), sem((steps,)), sem((steps,)), sem((steps,)), sem((steps,)), sem((steps,)),
        ],
        compiler_params=pltpu.CompilerParams(
            collective_id=0, has_side_effects=True, vmem_limit_bytes=67_000_000
        ),
    )(amplitudes, integrals.reshape(2, depth // 2, width))


def solution(mesh):
    placed = (P(("row", "col"), None), P("row", "col"))
    return jax.shard_map(
        body, mesh=mesh, in_specs=placed, out_specs=P(("row", "col"), None), check_vma=False
    )
```

time: 425 us -> 205 us (0.48)
  waiting for transfers between devices: 206 us -> 0 us
  Pallas kernels: 0 us -> 195 us
  blocking collectives: 167 us -> 0 us
  matrix products: 31.3 us -> 0 us
  between operations: 13.4 us -> 0.01 us
    all_gather x2 -> x0, waiting for transfers between devices: 205 us -> none  [the longest x1 130 us: body(): columns = lax.all_gather(integrals, 'row', axis=0, tiled=True)]
    pallas_call x0 -> x1, Pallas kernels: none -> 195 us  [body(): pl.pallas_call(functools.partial(kernel, steps), out_shape=jax.ShapeDtype...]
    all_to_all x2 -> x0, blocking collectives: 167 us -> none  [the longest x1 147 us: body(): lax.all_to_all(rounded, 'col', split_axis=0, concat_axis=1, tiled=True)]
    dot_general x1 -> x0, matrix products: 31.3 us -> none  [body(): jnp.dot(lax.all_gather(block_amps, 'col', axis=1, tiled=True), columns, p...]
    unnamed x1, local copies, waits for them, and re-layouts: 1.31 us -> 10.5 us
    all_to_all x2 -> x0, local copies, waits for them, and re-layouts: 6.18 us -> none  [the longest x1 5.17 us: body(): lax.all_to_all(rounded, 'col', split_axis=0, concat_axis=1, tiled=True)]
  transfers between devices with their start and end apart: 2 -> 0, of which waited for: 2 -> 0; matrix products, arithmetic and copies ran while one was open for 0% -> 0% of each run, Pallas kernels for 0% -> 0%
where the time goes in v1:
time: 205 us
  Pallas kernels  195 us (95%)
  local copies, waits for them, and re-layouts  10.5 us (5%)
    pallas_call x1, Pallas kernels, body(): pl.pallas_call(functools.partial(kernel, steps), out_shape=jax.ShapeDtype...  195 us
    unnamed x1, local copies, waits for them, and re-layouts  10.5 us

profile of v1, /device:TPU:1, one launch (start us, length us, event | category | flops | bytes accessed | tf_op | source)
XLA Modules:
  0.0 205.3 jit_solution(816343575051148702)
XLA Ops:
  0.0 194.8 %shard_map.28 = bf16[128,49152]{1,0:T(8,128)(2,1)} custom-call(bf16[128,2048]{1,0:T(8,128)(2,1)} %amps.1, bf16[2,128,3072]{2,1,0:T(8,128)(2,1)} %bitcast.1), custom_call_target="tpu_custom_call" | custom-call | tf_op jit(solution)/shard_map/pallas_call | solution.py:162
  194.8 10.5 %copy.4 = bf16[128,49152]{1,0:T(8,128)(2,1)} copy(bf16[128,49152]{1,0:T(8,128)(2,1)} %shard_map.28) | data formatting | bytes 25165824

commit v2 on v1

--- a/solution.py
+++ b/solution.py
@@ -8,7 +8,8 @@
 from jax.sharding import PartitionSpec as P
 
 MESH = pl.DeviceIdType.MESH
-W = 128
+W = 256
+PARTS = 8
 
 
 def kernel(steps, amps, ints, out, a_all, b_all, o_all, a_near, a_far, a_core, a_send, b_one, b_two, b_three, b_send, o_recv, o_send):
@@ -155,13 +156,22 @@
     lax.fori_loop(0, steps, drain, 0)
 
 
+def emit(src, dst, sem):
+    rows = src.shape[0] // PARTS
+    copies = [pltpu.make_async_copy(src.at[pl.ds(i * rows, rows)], dst.at[pl.ds(i * rows, rows)], sem.at[i]) for i in range(PARTS)]
+    for copy in copies:
+        copy.start()
+    for copy in copies:
+        copy.wait()
+
+
 def body(amplitudes, integrals):
     depth, width = integrals.shape
     steps = width // W
     sem = pltpu.SemaphoreType.DMA
-    return pl.pallas_call(
+    held = pl.pallas_call(
         functools.partial(kernel, steps),
-        out_shape=jax.ShapeDtypeStruct((128, 16 * width), jnp.bfloat16),
+        out_shape=pltpu.VMEM((128, 16 * width), jnp.bfloat16),
         in_specs=[pl.BlockSpec(memory_space=pl.ANY)] * 2,
         out_specs=pl.BlockSpec(memory_space=pl.ANY),
         scratch_shapes=[
@@ -172,9 +182,17 @@
             sem((steps,)), sem((steps,)), sem((steps,)), sem((steps,)), sem((steps,)), sem((steps,)),
         ],
         compiler_params=pltpu.CompilerParams(
-            collective_id=0, has_side_effects=True, vmem_limit_bytes=67_000_000
+            collective_id=0, has_side_effects=True, vmem_limit_bytes=54000000
         ),
     )(amplitudes, integrals.reshape(2, depth // 2, width))
+    return pl.pallas_call(
+        emit,
+        out_shape=jax.ShapeDtypeStruct(held.shape, held.dtype),
+        in_specs=[pl.BlockSpec(memory_space=pltpu.VMEM)],
+        out_specs=pl.BlockSpec(memory_space=pl.ANY),
+        scratch_shapes=[sem((PARTS,))],
+        compiler_params=pltpu.CompilerParams(vmem_limit_bytes=1_000_000),
+    )(held)
 
 
 def solution(mesh):

time: 205 us -> 181 us (0.88)
  Pallas kernels: 195 us -> 181 us
  local copies, waits for them, and re-layouts: 10.5 us -> 0 us
    pallas_call x1 -> x2, Pallas kernels: 195 us -> 181 us  [the longest x1 176 us: body(): pl.pallas_call(functools.partial(kernel, steps), out_shape=pltpu.VMEM((12...]
    unnamed x1 -> x0, local copies, waits for them, and re-layouts: 10.5 us -> none
where the time goes in v2:
time: 181 us
  Pallas kernels  181 us (100%)
    pallas_call x1, Pallas kernels, body(): pl.pallas_call(functools.partial(kernel, steps), out_shape=pltpu.VMEM((12...  176 us
    pallas_call x1, Pallas kernels, body(): pl.pallas_call(emit, out_shape=jax.ShapeDtypeStruct(held.shape, held.dtyp...  4.66 us

profile of v2, /device:TPU:1, one launch (start us, length us, event | category | flops | bytes accessed | tf_op | source)
XLA Modules:
  0.0 180.5 jit_solution(6123160840724311207)
XLA Ops:
  0.0 175.9 %shard_map.28.src = bf16[128,49152]{1,0:T(8,128)(2,1)S(1)} custom-call(bf16[128,2048]{1,0:T(8,128)(2,1)} %amps.1, bf16[2,128,3072]{2,1,0:T(8,128)(2,1)} %bitcast.1), custom_call_target="tpu_custom_call" | custom-call | tf_op jit(solution)/shard_map/pallas_call | solution.py:172
  175.9 4.7 %shard_map.29 = bf16[128,49152]{1,0:T(8,128)(2,1)} custom-call(bf16[128,49152]{1,0:T(8,128)(2,1)S(1)} %shard_map.28.src), custom_call_target="tpu_custom_call" | custom-call | tf_op jit(solution)/shard_map/pallas_call | solution.py:188

commit v3 on v0

v3 whole, which is shorter than its diff:
```python
import functools

import jax
import jax.numpy as jnp
from jax import lax
from jax.experimental import pallas as pl
from jax.experimental.pallas import tpu as pltpu
from jax.sharding import PartitionSpec as P

MESH = pl.DeviceIdType.MESH
PARTS = 8
HEAD, REST = (1, 256), (11, 256)


class Phase:
    def __init__(self, shape, first, start, refs):
        self.steps, self.w = shape
        self.first, self.start = first, start
        self.b, self.o, self.one, self.on, self.two, self.three, self.b_send, self.o_recv, self.o_send = refs

    def cols(self, j, base=0):
        return pl.ds(pl.multiple_of(base + self.start + j * self.w, 128), self.w)

    def block(self, h):
        return pl.ds(pl.multiple_of(h * self.w, self.w), self.w)


def kernel(amps, ints, out, a_all, a_near, a_far, a_own, a_core_near, a_core_far, a_send, *refs):
    row, col = lax.axis_index("row"), lax.axis_index("col")
    hi, lo, y, z, core = col // 8, row // 4, (col // 2) % 4, row % 4, col % 2
    x = hi * 2 + lo
    width = ints.shape[2]
    phases = [Phase(HEAD, 0, 0, refs[:9]), Phase(REST, HEAD[0], HEAD[0] * HEAD[1], refs[9:])]
    total = HEAD[0] + REST[0]

    def at(x, y, z, core):
        return ((x % 2) * 4 + z, (x // 2) * 8 + y * 2 + core)

    def turn(v, by):
        return (v + by) % 4

    def send(src, dst, send_sem, recv_sem, device):
        pltpu.make_async_remote_copy(
            src_ref=src, dst_ref=dst, send_sem=send_sem, recv_sem=recv_sem, device_id=device, device_id_type=MESH
        ).start()

    def await_bytes(ref, sem):
        pltpu.make_async_copy(ref, ref, sem).wait()

    barrier = pltpu.get_barrier_semaphore()
    ring = [1, 3, 2]
    partners = [at(turn(x, d), y, z, core) for d in (1, 3)] + [at(x, y, turn(z, d), core) for d in (1, 3)]
    partners += [at(x, turn(y, d), z, core) for d in ring] + [at(x, turn(y, d), z, 1 - core) for d in [0] + ring]
    for device in partners:
        pl.semaphore_signal(barrier, inc=1, device_id=device, device_id_type=MESH)
    pl.semaphore_wait(barrier, len(partners))

    def one(p, j):
        for d in (1, 3):
            send(ints.at[0, :, p.cols(j)], p.b.at[j, lo, z, 0, :, p.block(hi)], p.b_send.at[j], p.one.at[j], at(turn(x, d), y, z, core))
            send(ints.at[1, :, p.cols(j)], p.b.at[j, lo, z, 1, :, p.block(hi)], p.b_send.at[j], p.one.at[j], at(x, y, turn(z, d), core))
        pltpu.make_async_copy(ints.at[:, :, p.cols(j)], p.b.at[j, lo, z, :, :, p.block(hi)], p.one.at[j]).start()

    def on(p, j):
        await_bytes(p.b.at[j, 0, pl.ds(0, 3), 0], p.one.at[j])
        for i, d in enumerate((1, 3)):
            source = turn(x, 4 - d)
            block = p.b.at[j, source % 2, z, 0, pl.ds(64 * i, 64), p.block(source // 2)]
            send(block, block, p.b_send.at[j], p.on.at[j], at(turn(x, d), y, z, core))
            block = p.b.at[j, lo, turn(z, 4 - d), 1, pl.ds(64 * i, 64), p.block(hi)]
            send(block, block, p.b_send.at[j], p.on.at[j], at(x, y, turn(z, d), core))

    def two(p, j):
        await_bytes(p.b.at[j, 0, 0, 0], p.on.at[j])
        for d in (1, 3):
            block = p.b.at[j, :, z, 0]
            send(block, block, p.b_send.at[j], p.two.at[j], at(x, y, turn(z, d), core))
            block = p.b.at[j, lo, :, 1, :, p.block(hi)]
            send(block, block, p.b_send.at[j], p.two.at[j], at(turn(x, d), y, z, core))

    def three(p, j):
        await_bytes(p.b.at[j, :, :, 0], p.two.at[j])
        for i, d in enumerate((1, 3)):
            block = p.b.at[j, i, turn(z, 4 - d), 0]
            send(block, block, p.b_send.at[j], p.three.at[j], at(x, y, turn(z, d), core))
            source = turn(x, 4 - d)
            block = p.b.at[j, source % 2, pl.ds(2 * i, 2), 1, :, p.block(source // 2)]
            send(block, block, p.b_send.at[j], p.three.at[j], at(turn(x, d), y, z, core))

    def deliver(p, j, y_to):
        for k in range(2):
            for h in range(2):
                src = p.o.at[j, y_to, pl.ds(k * 128, 128), pl.ds(h * p.w, p.w)]
                dst = out.at[:, p.cols(j, (h * 8 + y * 2 + core) * width)]
                own = jnp.logical_and(y_to == y, core == k)

                @pl.when(own)
                def _():
                    pltpu.make_async_copy(src, dst, p.o_recv.at[j]).start()

                @pl.when(jnp.logical_not(own))
                def _():
                    send(src, dst, p.o_send.at[j], p.o_recv.at[j], at(x, y_to, z, k))

    def arrived(p, j):
        await_bytes(p.b.at[j, 0, :, 0], p.three.at[j])

    def compute(p, j):
        arrived(p, j)
        tiles(p, j, 0, 4)

    def tiles(p, j, first, last):
        def tile(m, _):
            y_to = turn(y, jnp.where(m == 0, 1, jnp.where(m == 1, 3, jnp.where(m == 2, 0, 2))))
            block = jnp.dot(
                a_all[pl.ds(2 * y_to, 2)].reshape(256, 2048),
                p.b[j].reshape(16 * 128, 2 * p.w),
                preferred_element_type=jnp.float32,
            )
            p.o[j, y_to] = block.astype(jnp.bfloat16)
            deliver(p, j, y_to)
            return 0

        lax.fori_loop(first, last, tile, 0)

    def to_core(y_of, sem):
        block = a_all.at[2 * y_of + core]
        send(block, block, a_send, sem, at(x, y, z, 1 - core))

    def amplitudes_start():
        mine = a_all.at[2 * y + core]
        send(amps, mine, a_send, a_near, at(x, turn(y, 1), z, core))
        send(amps, mine, a_send, a_near, at(x, turn(y, 3), z, core))
        send(amps, mine, a_send, a_own, at(x, y, z, 1 - core))
        pltpu.make_async_copy(amps, mine, a_own).start()

    def amplitudes_near():
        await_bytes(a_all.at[pl.ds(0, 2)], a_near)
        for i, d in enumerate((1, 3)):
            block = a_all.at[2 * turn(y, 4 - d) + core, pl.ds(64 * i, 64)]
            send(block, block, a_send, a_far, at(x, turn(y, d), z, core))
        to_core(turn(y, 1), a_core_near)
        to_core(turn(y, 3), a_core_near)
        await_bytes(a_all.at[pl.ds(0, 2)], a_own)
        await_bytes(a_all.at[pl.ds(0, 2)], a_core_near)

    def amplitudes_far():
        await_bytes(a_all.at[0], a_far)
        to_core(turn(y, 2), a_core_far)
        await_bytes(a_all.at[0], a_core_far)

    def stage(work, j):
        for p in phases:

            @pl.when(jnp.logical_and(j >= p.first, j < p.first + p.steps))
            def _():
                work(p, j - p.first)

    def step(t, _):
        @pl.when(t == 4)
        def _():
            amplitudes_near()
            arrived(phases[0], 0)
            tiles(phases[0], 0, 0, 3)

        stage(three, t - 3)
        stage(two, t - 2)
        stage(on, t - 1)
        stage(one, t)

        @pl.when(t == 0)
        def _():
            amplitudes_start()

        @pl.when(t == 4)
        def _():
            amplitudes_far()
            tiles(phases[0], 0, 3, 4)

        @pl.when(t > 4)
        def _():
            stage(compute, t - 4)

        return 0

    lax.fori_loop(0, total + 4, step, 0)

    await_bytes(a_all.at[pl.ds(0, 7)], a_send)

    for p in phases:

        def drain(j, _):
            await_bytes(out.at[:, pl.ds(0, 30 * p.w)], p.b_send.at[j])
            await_bytes(out.at[pl.ds(0, 112), pl.ds(0, 16 * p.w)], p.o_send.at[j])
            await_bytes(out.at[:, pl.ds(0, 16 * p.w)], p.o_recv.at[j])
            return 0

        lax.fori_loop(0, p.steps, drain, 0)


def emit(src, dst, sem):
    rows = src.shape[0] // PARTS
    copies = [pltpu.make_async_copy(src.at[pl.ds(i * rows, rows)], dst.at[pl.ds(i * rows, rows)], sem.at[i]) for i in range(PARTS)]
    for copy in copies:
        copy.start()
    for copy in copies:
        copy.wait()


def body(amplitudes, integrals):
    depth, width = integrals.shape
    sem = pltpu.SemaphoreType.DMA
    scratch = [pltpu.VMEM((8, 128, 2048), jnp.bfloat16)] + [sem] * 6
    for steps, w in (HEAD, REST):
        scratch += [
            pltpu.VMEM((steps, 2, 4, 2, 128, 2 * w), jnp.bfloat16),
            pltpu.VMEM((steps, 4, 256, 2 * w), jnp.bfloat16),
        ] + [sem((steps,))] * 7
    held = pl.pallas_call(
        kernel,
        out_shape=pltpu.VMEM((128, 16 * width), jnp.bfloat16),
        in_specs=[pl.BlockSpec(memory_space=pl.ANY)] * 2,
        out_specs=pl.BlockSpec(memory_space=pl.ANY),
        scratch_shapes=scratch,
        compiler_params=pltpu.CompilerParams(
            collective_id=0, has_side_effects=True, vmem_limit_bytes=54_000_000
        ),
    )(amplitudes, integrals.reshape(2, depth // 2, width))
    return pl.pallas_call(
        emit,
        out_shape=jax.ShapeDtypeStruct(held.shape, held.dtype),
        in_specs=[pl.BlockSpec(memory_space=pltpu.VMEM)],
        out_specs=pl.BlockSpec(memory_space=pl.ANY),
        scratch_shapes=[sem((PARTS,))],
        compiler_params=pltpu.CompilerParams(vmem_limit_bytes=1_000_000),
    )(held)


def solution(mesh):
    placed = (P(("row", "col"), None), P("row", "col"))
    return jax.shard_map(
        body, mesh=mesh, in_specs=placed, out_specs=P(("row", "col"), None), check_vma=False
    )
```

time: 425 us -> 174 us (0.41)
  waiting for transfers between devices: 206 us -> 0 us
  Pallas kernels: 0 us -> 174 us
  blocking collectives: 167 us -> 0 us
  matrix products: 31.3 us -> 0 us
  between operations: 13.4 us -> 0.01 us
  local copies, waits for them, and re-layouts: 7.48 us -> 0 us
    all_gather x2 -> x0, waiting for transfers between devices: 205 us -> none  [the longest x1 130 us: body(): columns = lax.all_gather(integrals, 'row', axis=0, tiled=True)]
    pallas_call x0 -> x2, Pallas kernels: none -> 174 us  [the longest x1 169 us: body(): pl.pallas_call(kernel, out_shape=pltpu.VMEM((128, 16 * width), jnp.bfloat...]
    all_to_all x2 -> x0, blocking collectives: 167 us -> none  [the longest x1 147 us: body(): lax.all_to_all(rounded, 'col', split_axis=0, concat_axis=1, tiled=True)]
    dot_general x1 -> x0, matrix products: 31.3 us -> none  [body(): jnp.dot(lax.all_gather(block_amps, 'col', axis=1, tiled=True), columns, p...]
    all_to_all x2 -> x0, local copies, waits for them, and re-layouts: 6.18 us -> none  [the longest x1 5.17 us: body(): lax.all_to_all(rounded, 'col', split_axis=0, concat_axis=1, tiled=True)]
  transfers between devices with their start and end apart: 2 -> 0, of which waited for: 2 -> 0; matrix products, arithmetic and copies ran while one was open for 0% -> 0% of each run, Pallas kernels for 0% -> 0%
where the time goes in v3:
time: 174 us
  Pallas kernels  174 us (100%)
    pallas_call x1, Pallas kernels, body(): pl.pallas_call(kernel, out_shape=pltpu.VMEM((128, 16 * width), jnp.bfloat...  169 us
    pallas_call x1, Pallas kernels, body(): pl.pallas_call(emit, out_shape=jax.ShapeDtypeStruct(held.shape, held.dtyp...  4.66 us

profile of v3, /device:TPU:1, one launch (start us, length us, event | category | flops | bytes accessed | tf_op | source)
XLA Modules:
  0.0 173.7 jit_solution(4616922021904565524)
XLA Ops:
  0.0 169.0 %shard_map.28.src = bf16[128,49152]{1,0:T(8,128)(2,1)S(1)} custom-call(bf16[128,2048]{1,0:T(8,128)(2,1)} %amps.1, bf16[2,128,3072]{2,1,0:T(8,128)(2,1)} %bitcast.1), custom_call_target="tpu_custom_call" | custom-call | tf_op jit(solution)/shard_map/pallas_call | solution.py:219
  169.0 4.7 %shard_map.29 = bf16[128,49152]{1,0:T(8,128)(2,1)} custom-call(bf16[128,49152]{1,0:T(8,128)(2,1)S(1)} %shard_map.28.src), custom_call_target="tpu_custom_call" | custom-call | tf_op jit(solution)/shard_map/pallas_call | solution.py:229

commit v4 on v3

--- a/solution.py
+++ b/solution.py
@@ -9,14 +9,14 @@
 
 MESH = pl.DeviceIdType.MESH
 PARTS = 8
-HEAD, REST = (1, 256), (11, 256)
+HEAD, REST = (1, 128), (23, 128)
 
 
 class Phase:
     def __init__(self, shape, first, start, refs):
         self.steps, self.w = shape
         self.first, self.start = first, start
-        self.b, self.o, self.one, self.on, self.two, self.three, self.b_send, self.o_recv, self.o_send = refs
+        self.b, self.o, self.one, self.rest_one, self.on, self.two, self.rest_two, self.three, self.b_send, self.o_recv, self.o_send = refs
 
     def cols(self, j, base=0):
         return pl.ds(pl.multiple_of(base + self.start + j * self.w, 128), self.w)
@@ -25,12 +25,12 @@
         return pl.ds(pl.multiple_of(h * self.w, self.w), self.w)
 
 
-def kernel(amps, ints, out, a_all, a_near, a_far, a_own, a_core_near, a_core_far, a_send, *refs):
+def kernel(amps, ints, out, a_all, a_first, a_second, a_far, a_own, a_core_near, a_core_far, a_send, *refs):
     row, col = lax.axis_index("row"), lax.axis_index("col")
     hi, lo, y, z, core = col // 8, row // 4, (col // 2) % 4, row % 4, col % 2
     x = hi * 2 + lo
     width = ints.shape[2]
-    phases = [Phase(HEAD, 0, 0, refs[:9]), Phase(REST, HEAD[0], HEAD[0] * HEAD[1], refs[9:])]
+    phases = [Phase(HEAD, 0, 0, refs[:11]), Phase(REST, HEAD[0], HEAD[0] * HEAD[1], refs[11:])]
     total = HEAD[0] + REST[0]
 
     def at(x, y, z, core):
@@ -56,13 +56,15 @@
     pl.semaphore_wait(barrier, len(partners))
 
     def one(p, j):
-        for d in (1, 3):
-            send(ints.at[0, :, p.cols(j)], p.b.at[j, lo, z, 0, :, p.block(hi)], p.b_send.at[j], p.one.at[j], at(turn(x, d), y, z, core))
-            send(ints.at[1, :, p.cols(j)], p.b.at[j, lo, z, 1, :, p.block(hi)], p.b_send.at[j], p.one.at[j], at(x, y, turn(z, d), core))
-        pltpu.make_async_copy(ints.at[:, :, p.cols(j)], p.b.at[j, lo, z, :, :, p.block(hi)], p.one.at[j]).start()
+        for sem, flip in ((p.one, 0), (p.rest_one, 1)):
+            for i, d in enumerate((1, 3)):
+                rows = pl.ds(64 * (i ^ flip), 64)
+                send(ints.at[0, rows, p.cols(j)], p.b.at[j, lo, z, 0, rows, p.block(hi)], p.b_send.at[j], sem.at[j], at(turn(x, d), y, z, core))
+                send(ints.at[1, rows, p.cols(j)], p.b.at[j, lo, z, 1, rows, p.block(hi)], p.b_send.at[j], sem.at[j], at(x, y, turn(z, d), core))
+        pltpu.make_async_copy(ints.at[:, :, p.cols(j)], p.b.at[j, lo, z, :, :, p.block(hi)], p.rest_one.at[j]).start()
 
     def on(p, j):
-        await_bytes(p.b.at[j, 0, pl.ds(0, 3), 0], p.one.at[j])
+        await_bytes(p.b.at[j, 0, 0, 0], p.one.at[j])
         for i, d in enumerate((1, 3)):
             source = turn(x, 4 - d)
             block = p.b.at[j, source % 2, z, 0, pl.ds(64 * i, 64), p.block(source // 2)]
@@ -71,15 +73,17 @@
             send(block, block, p.b_send.at[j], p.on.at[j], at(x, y, turn(z, d), core))
 
     def two(p, j):
+        await_bytes(p.b.at[j, 0, pl.ds(0, 2), 0], p.rest_one.at[j])
         await_bytes(p.b.at[j, 0, 0, 0], p.on.at[j])
-        for d in (1, 3):
-            block = p.b.at[j, :, z, 0]
-            send(block, block, p.b_send.at[j], p.two.at[j], at(x, y, turn(z, d), core))
-            block = p.b.at[j, lo, :, 1, :, p.block(hi)]
-            send(block, block, p.b_send.at[j], p.two.at[j], at(turn(x, d), y, z, core))
+        for sem, flip in ((p.two, 0), (p.rest_two, 1)):
+            for i, d in enumerate((1, 3)):
+                block = p.b.at[j, i ^ flip, z, 0]
+                send(block, block, p.b_send.at[j], sem.at[j], at(x, y, turn(z, d), core))
+                block = p.b.at[j, lo, pl.ds(2 * (i ^ flip), 2), 1, :, p.block(hi)]
+                send(block, block, p.b_send.at[j], sem.at[j], at(turn(x, d), y, z, core))
 
     def three(p, j):
-        await_bytes(p.b.at[j, :, :, 0], p.two.at[j])
+        await_bytes(p.b.at[j, 0, :, 0], p.two.at[j])
         for i, d in enumerate((1, 3)):
             block = p.b.at[j, i, turn(z, 4 - d), 0]
             send(block, block, p.b_send.at[j], p.three.at[j], at(x, y, turn(z, d), core))
@@ -103,6 +107,7 @@
                     send(src, dst, p.o_send.at[j], p.o_recv.at[j], at(x, y_to, z, k))
 
     def arrived(p, j):
+        await_bytes(p.b.at[j, 0, :, 0], p.rest_two.at[j])
         await_bytes(p.b.at[j, 0, :, 0], p.three.at[j])
 
     def compute(p, j):
@@ -129,18 +134,25 @@
 
     def amplitudes_start():
         mine = a_all.at[2 * y + core]
-        send(amps, mine, a_send, a_near, at(x, turn(y, 1), z, core))
-        send(amps, mine, a_send, a_near, at(x, turn(y, 3), z, core))
+        for sem, flip in ((a_first, 0), (a_second, 1)):
+            for i, d in enumerate((1, 3)):
+                rows = pl.ds(64 * (i ^ flip), 64)
+                send(amps.at[rows], mine.at[rows], a_send, sem, at(x, turn(y, d), z, core))
         send(amps, mine, a_send, a_own, at(x, y, z, 1 - core))
         pltpu.make_async_copy(amps, mine, a_own).start()
 
-    def amplitudes_near():
-        await_bytes(a_all.at[pl.ds(0, 2)], a_near)
+    def amplitudes_on():
+        await_bytes(a_all.at[0], a_first)
         for i, d in enumerate((1, 3)):
             block = a_all.at[2 * turn(y, 4 - d) + core, pl.ds(64 * i, 64)]
             send(block, block, a_send, a_far, at(x, turn(y, d), z, core))
+
+    def amplitudes_near():
+        await_bytes(a_all.at[0], a_second)
         to_core(turn(y, 1), a_core_near)
         to_core(turn(y, 3), a_core_near)
+
+    def amplitudes_ready():
         await_bytes(a_all.at[pl.ds(0, 2)], a_own)
         await_bytes(a_all.at[pl.ds(0, 2)], a_core_near)
 
@@ -159,7 +171,7 @@
     def step(t, _):
         @pl.when(t == 4)
         def _():
-            amplitudes_near()
+            amplitudes_ready()
             arrived(phases[0], 0)
             tiles(phases[0], 0, 0, 3)
 
@@ -171,6 +183,14 @@
         @pl.when(t == 0)
         def _():
             amplitudes_start()
+
+        @pl.when(t == 2)
+        def _():
+            amplitudes_on()
+
+        @pl.when(t == 3)
+        def _():
+            amplitudes_near()
 
         @pl.when(t == 4)
         def _():
@@ -210,12 +230,12 @@
 def body(amplitudes, integrals):
     depth, width = integrals.shape
     sem = pltpu.SemaphoreType.DMA
-    scratch = [pltpu.VMEM((8, 128, 2048), jnp.bfloat16)] + [sem] * 6
+    scratch = [pltpu.VMEM((8, 128, 2048), jnp.bfloat16)] + [sem] * 7
     for steps, w in (HEAD, REST):
         scratch += [
             pltpu.VMEM((steps, 2, 4, 2, 128, 2 * w), jnp.bfloat16),
             pltpu.VMEM((steps, 4, 256, 2 * w), jnp.bfloat16),
-        ] + [sem((steps,))] * 7
+        ] + [sem((steps,))] * 9
     held = pl.pallas_call(
         kernel,
         out_shape=pltpu.VMEM((128, 16 * width), jnp.bfloat16),

time: 174 us -> 173 us (level)
  no operation moved by 1% of the time
where the time goes in v4:
time: 173 us
  Pallas kernels  173 us (100%)
    pallas_call x1, Pallas kernels, body(): pl.pallas_call(kernel, out_shape=pltpu.VMEM((128, 16 * width), jnp.bfloat...  168 us
    pallas_call x1, Pallas kernels, body(): pl.pallas_call(emit, out_shape=jax.ShapeDtypeStruct(held.shape, held.dtyp...  4.66 us

profile of v4, /device:TPU:1, one launch (start us, length us, event | category | flops | bytes accessed | tf_op | source)
XLA Modules:
  0.0 173.0 jit_solution(12779448765257076966)
XLA Ops:
  0.0 168.3 %shard_map.28.src = bf16[128,49152]{1,0:T(8,128)(2,1)S(1)} custom-call(bf16[128,2048]{1,0:T(8,128)(2,1)} %amps.1, bf16[2,128,3072]{2,1,0:T(8,128)(2,1)} %bitcast.1), custom_call_target="tpu_custom_call" | custom-call | tf_op jit(solution)/shard_map/pallas_call | solution.py:239
  168.3 4.7 %shard_map.29 = bf16[128,49152]{1,0:T(8,128)(2,1)} custom-call(bf16[128,49152]{1,0:T(8,128)(2,1)S(1)} %shard_map.28.src), custom_call_target="tpu_custom_call" | custom-call | tf_op jit(solution)/shard_map/pallas_call | solution.py:249

commit v5 on v4

--- a/solution.py
+++ b/solution.py
@@ -1,5 +1,3 @@
-import functools
-
 import jax
 import jax.numpy as jnp
 from jax import lax
@@ -8,7 +6,7 @@
 from jax.sharding import PartitionSpec as P
 
 MESH = pl.DeviceIdType.MESH
-PARTS = 8
+GROUP, LAG = 4, 16
 HEAD, REST = (1, 128), (23, 128)
 
 
@@ -25,7 +23,7 @@
         return pl.ds(pl.multiple_of(h * self.w, self.w), self.w)
 
 
-def kernel(amps, ints, out, a_all, a_first, a_second, a_far, a_own, a_core_near, a_core_far, a_send, *refs):
+def kernel(amps, ints, out, held, written, a_all, a_first, a_second, a_far, a_own, a_core_near, a_core_far, a_send, *refs):
     row, col = lax.axis_index("row"), lax.axis_index("col")
     hi, lo, y, z, core = col // 8, row // 4, (col // 2) % 4, row % 4, col % 2
     x = hi * 2 + lo
@@ -95,7 +93,7 @@
         for k in range(2):
             for h in range(2):
                 src = p.o.at[j, y_to, pl.ds(k * 128, 128), pl.ds(h * p.w, p.w)]
-                dst = out.at[:, p.cols(j, (h * 8 + y * 2 + core) * width)]
+                dst = held.at[:, p.cols(j, (h * 8 + y * 2 + core) * width)]
                 own = jnp.logical_and(y_to == y, core == k)
 
                 @pl.when(own)
@@ -168,6 +166,16 @@
             def _():
                 work(p, j - p.first)
 
+    def landed(p, j):
+        await_bytes(held.at[:, pl.ds(0, 16 * p.w)], p.o_recv.at[j])
+
+    def write(first, steps):
+        for i in range(steps):
+            stage(landed, first + i)
+        for c in range(16):
+            cols = pl.ds(pl.multiple_of(c * width + first * 128, 128), steps * 128)
+            pltpu.make_async_copy(held.at[:, cols], out.at[:, cols], written).start()
+
     def step(t, _):
         @pl.when(t == 4)
         def _():
@@ -201,59 +209,52 @@
         def _():
             stage(compute, t - 4)
 
+        @pl.when(jnp.logical_and(t >= LAG, t % GROUP == 0))
+        def _():
+            write(t - LAG, GROUP)
+
         return 0
 
     lax.fori_loop(0, total + 4, step, 0)
+    late = range(LAG, total + 4, GROUP)[-1] - LAG + GROUP
+    for first in range(late, total - GROUP, GROUP):
+        write(first, GROUP)
+    for first in range(total - GROUP, total):
+        write(first, 1)
 
     await_bytes(a_all.at[pl.ds(0, 7)], a_send)
 
     for p in phases:
 
         def drain(j, _):
-            await_bytes(out.at[:, pl.ds(0, 30 * p.w)], p.b_send.at[j])
-            await_bytes(out.at[pl.ds(0, 112), pl.ds(0, 16 * p.w)], p.o_send.at[j])
-            await_bytes(out.at[:, pl.ds(0, 16 * p.w)], p.o_recv.at[j])
+            await_bytes(held.at[:, pl.ds(0, 30 * p.w)], p.b_send.at[j])
+            await_bytes(held.at[pl.ds(0, 112), pl.ds(0, 16 * p.w)], p.o_send.at[j])
             return 0
 
         lax.fori_loop(0, p.steps, drain, 0)
 
-
-def emit(src, dst, sem):
-    rows = src.shape[0] // PARTS
-    copies = [pltpu.make_async_copy(src.at[pl.ds(i * rows, rows)], dst.at[pl.ds(i * rows, rows)], sem.at[i]) for i in range(PARTS)]
-    for copy in copies:
-        copy.start()
-    for copy in copies:
-        copy.wait()
+    await_bytes(held, written)
 
 
 def body(amplitudes, integrals):
     depth, width = integrals.shape
     sem = pltpu.SemaphoreType.DMA
-    scratch = [pltpu.VMEM((8, 128, 2048), jnp.bfloat16)] + [sem] * 7
+    scratch = [pltpu.VMEM((128, 16 * width), jnp.bfloat16), sem, pltpu.VMEM((8, 128, 2048), jnp.bfloat16)] + [sem] * 7
     for steps, w in (HEAD, REST):
         scratch += [
             pltpu.VMEM((steps, 2, 4, 2, 128, 2 * w), jnp.bfloat16),
             pltpu.VMEM((steps, 4, 256, 2 * w), jnp.bfloat16),
         ] + [sem((steps,))] * 9
-    held = pl.pallas_call(
+    return pl.pallas_call(
         kernel,
-        out_shape=pltpu.VMEM((128, 16 * width), jnp.bfloat16),
+        out_shape=jax.ShapeDtypeStruct((128, 16 * width), jnp.bfloat16),
         in_specs=[pl.BlockSpec(memory_space=pl.ANY)] * 2,
-        out_specs=pl.BlockSpec(memory_space=pl.ANY),
+        out_specs=pl.BlockSpec(memory_space=pltpu.HBM),
         scratch_shapes=scratch,
         compiler_params=pltpu.CompilerParams(
-            collective_id=0, has_side_effects=True, vmem_limit_bytes=54_000_000
+            collective_id=0, has_side_effects=True, vmem_limit_bytes=60_000_000
         ),
     )(amplitudes, integrals.reshape(2, depth // 2, width))
-    return pl.pallas_call(
-        emit,
-        out_shape=jax.ShapeDtypeStruct(held.shape, held.dtype),
-        in_specs=[pl.BlockSpec(memory_space=pltpu.VMEM)],
-        out_specs=pl.BlockSpec(memory_space=pl.ANY),
-        scratch_shapes=[sem((PARTS,))],
-        compiler_params=pltpu.CompilerParams(vmem_limit_bytes=1_000_000),
-    )(held)
 
 
 def solution(mesh):

time: 173 us -> 180 us (1.040)
  local copies, waits for them, and re-layouts: 0 us -> 10.5 us
  Pallas kernels: 173 us -> 169 us
    unnamed x0 -> x1, local copies, waits for them, and re-layouts: none -> 10.5 us
    pallas_call x2 -> x1, Pallas kernels: 173 us -> 169 us  [body(): pl.pallas_call(kernel, out_shape=jax.ShapeDtypeStruct((128, 16 * width),...]
where the time goes in v5:
time: 180 us
  Pallas kernels  169 us (94%)
  local copies, waits for them, and re-layouts  10.5 us (6%)
    pallas_call x1, Pallas kernels, body(): pl.pallas_call(kernel, out_shape=jax.ShapeDtypeStruct((128, 16 * width),...  169 us
    unnamed x1, local copies, waits for them, and re-layouts  10.5 us

profile of v5, /device:TPU:1, one launch (start us, length us, event | category | flops | bytes accessed | tf_op | source)
XLA Modules:
  0.0 179.7 jit_solution(13683073466654770199)
XLA Ops:
  0.0 169.3 %shard_map.28 = bf16[128,49152]{1,0:T(8,128)(2,1)} custom-call(bf16[128,2048]{1,0:T(8,128)(2,1)} %amps.1, bf16[2,128,3072]{2,1,0:T(8,128)(2,1)} %bitcast.1), custom_call_target="tpu_custom_call" | custom-call | tf_op jit(solution)/shard_map/pallas_call | solution.py:248
  169.3 10.5 %copy.4 = bf16[128,49152]{1,0:T(8,128)(2,1)} copy(bf16[128,49152]{1,0:T(8,128)(2,1)} %shard_map.28) | data formatting | bytes 25165824
